TPU v7x, 512 devices: a whole 4x4x16 slice. The times are simulated.
512 devices in a mesh: grp: 8 (over x, core), path: 64 (over z, y).
Axes of the slice: x: 4, y: 4, z: 16, core: 2. Of those that a mesh axis runs over, the one named last changes fastest.
Arguments:
- normals: float32 [32, 8388608], P(None, ('grp', 'path')), may hold values from -10.1 to 10.1
- spot_today: float32 [32], replicated, may hold values from 0.5 to 2
- volatility: float32 [32], replicated, may hold values from 0.1 to 0.5
- weights: float32 [32], replicated, may hold values from 0.5 to 1.5
- cash_flows: float32 [8388608], P(('grp', 'path')), may hold values from -300 to 300
- exercise: int32 [8388608], P(('grp', 'path')), may hold values 0 or 1
Outputs:
- path_value: float32 [8388608], P(('grp', 'path'))
- state_cot: float32 [32, 8388608], P(None, ('grp', 'path'))
- flow_cot: float32 [8388608], P(('grp', 'path'))
- greeks: float32 [2, 32], replicated
All inputs are finite; a program needn't handle non-finite values. No bound on the sum of `exercise` on one device may be relied on, other than what follows from the above.
Results may differ from a plain program's by a relative error of at most 0.0003.
Values sent between devices are 32-bit elements; how exact they have to be, the bound alone decides.
A program may use at most 64 MiB of HBM per device.

v0:
```python
import math
import jax
import jax.numpy as jnp
from jax import lax
from jax.sharding import PartitionSpec as P

expiry_time = 0.5
root_time = math.sqrt(0.5)
inv_root_two = 1.0 / math.sqrt(2.0)
notional = 20.0
soft_width = 0.02


def path_state(normals, spot_today, volatility):
    return spot_today[:, None] * jnp.exp(
        volatility[:, None] * (root_time * normals) - 0.5 * expiry_time * volatility[:, None] ** 2
    )


def basis_rows(state, spot_today, volatility):
    scaled = (state / spot_today[:, None] - 1.0) / (volatility[:, None] * root_time)
    leading = jnp.ones_like(scaled[:1])
    squares = (scaled * scaled - 1.0) * inv_root_two
    neighbour = scaled * jnp.roll(scaled, -1, axis=0)
    bounded = jnp.tanh(scaled[:-1])
    return jnp.concatenate([leading, scaled, squares, neighbour, bounded], axis=0)


def payoff(state, spot_today, weights):
    basket = jnp.sum(weights[:, None] * state, axis=0) / jnp.sum(weights * spot_today)
    return notional * soft_width * jax.nn.softplus((basket - 1.0) / soft_width)


def chol_solve(factor, rhs):
    first = lax.linalg.triangular_solve(factor, rhs, left_side=True, lower=True)
    return lax.linalg.triangular_solve(factor, first, left_side=True, lower=True, transpose_a=True)


def per_device(normals, spot_today, volatility, weights, cash_flows, exercise):
    assets, local_paths = normals.shape
    features = 4 * assets
    block_width = math.gcd(local_paths, 1024)
    block_count = local_paths // block_width
    path_total = local_paths * lax.axis_size("grp") * lax.axis_size("path")
    highest = lax.Precision.HIGHEST
    contract_last = (((1,), (1,)), ((), ()))

    def block_inputs(block_index):
        block_start = block_index * block_width
        draw_block = lax.dynamic_slice_in_dim(normals, block_start, block_width, 1)
        flow_block = lax.dynamic_slice_in_dim(cash_flows, block_start, block_width, 0)
        taken_flag = lax.dynamic_slice_in_dim(exercise, block_start, block_width, 0).astype(
            jnp.float32
        )
        return (draw_block, flow_block, taken_flag)

    def gram_step(block_index, running):
        gram_acc, moment_acc = running
        draw_block, flow_block, taken_flag = block_inputs(block_index)
        basis_block = basis_rows(
            path_state(draw_block, spot_today, volatility), spot_today, volatility
        )
        gram_acc = gram_acc + lax.dot_general(
            basis_block,
            basis_block,
            contract_last,
            precision=highest,
            preferred_element_type=jnp.float32,
        )
        targets = jnp.stack([flow_block, 1.0 - taken_flag])
        moment_acc = moment_acc + lax.dot_general(
            targets,
            basis_block,
            contract_last,
            precision=highest,
            preferred_element_type=jnp.float32,
        )
        return (gram_acc, moment_acc)

    zero_gram = jnp.zeros((features, features), jnp.float32)
    zero_moment = jnp.zeros((2, features), jnp.float32)
    gram_acc, moment_acc = lax.fori_loop(0, block_count, gram_step, (zero_gram, zero_moment))
    gram_sum, moment_sum = lax.psum((gram_acc, moment_acc), ("grp", "path"))
    gram_mean = gram_sum / path_total
    moment_mean = moment_sum / path_total
    factor = jnp.linalg.cholesky(gram_mean)
    coefficients = chol_solve(factor, moment_mean.T)
    regression = coefficients[:, 0]
    multiplier = coefficients[:, 1]
    coef_rows = coefficients.T

    def adjoint_step(block_index, running):
        value_out, state_out, flow_out, greek_acc = running
        draw_block, flow_block, taken_flag = block_inputs(block_index)
        state, path_back = jax.vjp(
            lambda spot_level, spread: path_state(draw_block, spot_level, spread),
            spot_today,
            volatility,
        )
        (basis_block, reward), feature_back = jax.vjp(
            lambda current, spot_level, spread: (
                basis_rows(current, spot_level, spread),
                payoff(current, spot_level, weights),
            ),
            state,
            spot_today,
            volatility,
        )
        fitted = lax.dot_general(
            coef_rows,
            basis_block,
            (((1,), (0,)), ((), ())),
            precision=highest,
            preferred_element_type=jnp.float32,
        )
        continuation = fitted[0]
        lam_phi = fitted[1]
        value_block = taken_flag * reward + (1.0 - taken_flag) * continuation
        rows_bar = (
            multiplier[:, None] * (flow_block - continuation)[None, :]
            + regression[:, None] * (1.0 - taken_flag - lam_phi)[None, :]
        )
        state_bar, spot_bar, spread_bar = feature_back((rows_bar, taken_flag))
        spot_path, spread_path = path_back(state_bar)
        greek_acc = greek_acc + jnp.stack([spot_bar + spot_path, spread_bar + spread_path])
        block_start = block_index * block_width
        value_out = lax.dynamic_update_slice_in_dim(value_out, value_block, block_start, 0)
        state_out = lax.dynamic_update_slice_in_dim(state_out, state_bar, block_start, 1)
        flow_out = lax.dynamic_update_slice_in_dim(flow_out, lam_phi, block_start, 0)
        return (value_out, state_out, flow_out, greek_acc)

    start_outs = (
        jnp.zeros((local_paths,), jnp.float32),
        jnp.zeros((assets, local_paths), jnp.float32),
        jnp.zeros((local_paths,), jnp.float32),
        jnp.zeros((2, assets), jnp.float32),
    )
    path_value, state_cot, flow_cot, greek_acc = lax.fori_loop(
        0, block_count, adjoint_step, start_outs
    )
    greeks = lax.psum(greek_acc, ("grp", "path")) / path_total
    return (path_value, state_cot, flow_cot, greeks)


def solution(mesh):
    in_specs = (P(None, ("grp", "path")), P(), P(), P(), P(("grp", "path")), P(("grp", "path")))
    out_specs = (P(("grp", "path")), P(None, ("grp", "path")), P(("grp", "path")), P())
    return jax.shard_map(
        per_device, mesh=mesh, in_specs=in_specs, out_specs=out_specs, check_vma=False
    )
```

profile of v0, /device:TPU:1, one launch (start us, length us, event | category | flops | bytes accessed | tf_op | source)
XLA Modules:
  0.0 799.2 jit_solution(2905008628798093460)
XLA Ops:
  7.9 80.4 %while.42 = (s32[]{:T(128)}, f32[128,128]{1,0:T(8,128)S(1)}, f32[2,128]{1,0:T(2,128)S(1)}, f32[32]{0:T(128)}, f32[32,16384]{1,0:T(8,128)}, /*index=5*/f32[32]{0:...) while((s32[]{:T(128)}, f32[128,128]{1,0:T(8,128)S(1)}, ...), condition=%wide.region_1.2_spmd.clone, body=%wide.region_0.1_spmd.clone.sunk | while | flops 204870208 | bytes 3562582 | solution.py:82
  89.1 1.3 multiply_bitcast_fusion.2
  91.7 111.2 %psum.22 = f32[2,128]{1,0:T(2,128)S(1)} all-reduce(f32[2,128]{1,0:T(2,128)S(1)} %get-tuple-element.642), channel_id=1, replica_groups=mesh['grp'=8,'path'=64] {'grp','path'}, use_global_device_ids=true, to_apply=%region_5.6 | all-reduce | flops 256 | bytes 2048 | tf_op jit(solution)/shard_map/psum | solution.py:83
  202.9 340.4 %all-reduce.5.cloned.1.call-done = f32[128,128]{0,1:T(8,128)} async-done(((f32[128,128]{0,1:T(8,128)}), f32[128,128]{0,1:T(8,128)}) %all-reduce.5.cloned.1.call-update) | async-done | bytes 65552 | tf_op jit(solution)/shard_map/psum | solution.py:83
  545.1 11.7 %cholesky.15 = f32[128,128]{1,0:T(8,128)S(1)} custom-call(f32[128,128]{1,0:T(8,128)S(1)} %fusion.19), custom_call_target="Cholesky" | custom-call | tf_op jit(solution)/shard_map/jit(cholesky)/cholesky | solution.py:86
  558.1 9.8 %custom-call.8 = f32[1,128,128]{1,2,0:T(8,128)S(1)} custom-call(f32[1,128,128]{2,1,0:T(8,128)S(1)} %fusion.14), custom_call_target="InvertDiagBlocksLowerTriangular" | custom-call | tf_op jit(solution)/shard_map/triangular_solve | solution.py:36
  568.7 121.5 %while.43 = (s32[]{:T(128)}, f32[16384]{0:T(1024)S(1)}, f32[32,16384]{1,0:T(8,128)S(1)}, f32[16384]{0:T(1024)S(1)}, f32[2,32]{1,0:T(2,128)S(1)}, /*index=5*/s32[...) while((s32[]{:T(128)}, f32[16384]{0:T(1024)S(1)}, ...), condition=%wide.region_15.16_spmd.clone, body=%wide.region_7.15_spmd.clone.sunk | while | flops 5333607 | bytes 5730625 | solution.py:138
  568.8 1.0 add_multiply_fusion.6
  571.3 2.0 multiply_reduce_fusion.8
  574.8 1.3 fusion.49
  576.4 1.0 add_multiply_fusion.6
  578.9 2.0 multiply_reduce_fusion.8
  582.4 1.3 fusion.49
  584.0 1.0 add_multiply_fusion.6
  586.5 2.0 multiply_reduce_fusion.8
  590.0 1.3 fusion.49
  591.6 1.0 add_multiply_fusion.6
  594.1 2.0 multiply_reduce_fusion.8
  597.6 1.3 fusion.49
  599.2 1.0 add_multiply_fusion.6
  601.7 2.0 multiply_reduce_fusion.8
  605.2 1.3 fusion.49
  606.7 1.0 add_multiply_fusion.6
  609.3 2.0 multiply_reduce_fusion.8
  612.8 1.3 fusion.49
  616.9 2.0 multiply_reduce_fusion.8
  620.4 1.3 fusion.49
  624.5 2.0 multiply_reduce_fusion.8
  628.0 1.3 fusion.49
  629.5 1.0 add_multiply_fusion.6
  632.1 2.0 multiply_reduce_fusion.8
  635.6 1.3 fusion.49
  639.7 2.0 multiply_reduce_fusion.8
  643.2 1.3 fusion.49
  647.3 2.0 multiply_reduce_fusion.8
  650.8 1.3 fusion.49
  654.9 2.0 multiply_reduce_fusion.8
  658.4 1.3 fusion.49
  662.5 2.0 multiply_reduce_fusion.8
  666.0 1.3 fusion.49
  667.5 1.0 add_multiply_fusion.6
  670.1 2.0 multiply_reduce_fusion.8
  673.6 1.3 fusion.49
  677.7 2.0 multiply_reduce_fusion.8
  681.2 1.3 fusion.49
  685.2 2.0 multiply_reduce_fusion.8
  688.8 1.3 fusion.49
  690.3 101.5 %psum.23 = f32[2,32]{1,0:T(2,128)S(1)} all-reduce(f32[2,32]{1,0:T(2,128)S(1)} %get-tuple-element.646), channel_id=1, replica_groups=mesh['grp'=8,'path'=64] {'grp','path'}, use_global_device_ids=true, to_apply=%region_16.17 | all-reduce | flops 64 | bytes 512 | tf_op jit(solution)/shard_map/psum | solution.py:141
  (536 shorter events, 131.8 us)
Async XLA Ops:
  7.2 536.1 %all-reduce.5.cloned.1.call-start = ((), (), s32[]{:S(2)}) async-start(), calls=%async_computation | async-start | bytes 131072 | tf_op jit(solution)/shard_map/psum | solution.py:83
  7.9 81.2 %copy-start.1 = (f32[32]{0:T(128)S(1)}, f32[32]{0:T(128)}, u32[]{:S(2)}) copy-start(f32[32]{0:T(128)} %param.13) | copy-start | bytes 388
  88.3 480.4 %copy-start.2 = (f32[32]{0:T(128)S(1)}, f32[32]{0:T(128)}, u32[]{:S(2)}) copy-start(f32[32]{0:T(128)} %get-tuple-element.1153) | copy-start | bytes 388
  88.3 480.4 %copy-start.5 = (f32[32]{0:T(128)S(1)}, f32[32]{0:T(128)}, u32[]{:S(2)}) copy-start(f32[32]{0:T(128)} %get-tuple-element.1154) | copy-start | bytes 388
  690.2 102.1 %copy-start = (f32[32,16384]{1,0:T(8,128)}, f32[32,16384]{1,0:T(8,128)S(1)}, u32[]{:S(2)}) copy-start(f32[32,16384]{1,0:T(8,128)S(1)} %get-tuple-element.638) | copy-start | bytes 6291460
  690.3 102.1 %copy-start.3 = (f32[16384]{0:T(1024)}, f32[16384]{0:T(1024)S(1)}, u32[]{:S(2)}) copy-start(f32[16384]{0:T(1024)S(1)} %get-tuple-element.639) | copy-start | bytes 196612
  690.3 102.1 %copy-start.4 = (f32[16384]{0:T(1024)}, f32[16384]{0:T(1024)S(1)}, u32[]{:S(2)}) copy-start(f32[16384]{0:T(1024)S(1)} %get-tuple-element.637) | copy-start | bytes 196612
Sparse Core Ops, SparseCore 0:
  89.2 454.0 all-reduce.4
where the time goes:
time: 803 us; the launch traced here: 799 us
  waiting for transfers between devices  340 us (42%)
  blocking collectives  213 us (27%)
  other arithmetic  151 us (19%)
  local copies, waits for them, and re-layouts  40.1 us (5%)
  matrix products  24.6 us (3%)
  between operations  15.5 us (2%)
  loops' own time  14.4 us (2%)
    psum x1, waiting for transfers between devices, per_device(): gram_sum, moment_sum = lax.psum((gram_acc, moment_acc), ('grp', 'path'))  340 us
    psum x1, blocking collectives, per_device(): gram_sum, moment_sum = lax.psum((gram_acc, moment_acc), ('grp', 'path'))  111 us
    psum x1, blocking collectives, per_device(): greeks = lax.psum(greek_acc, ('grp', 'path')) / path_total  101 us
    mul x32, other arithmetic, basis_rows(): squares = (scaled * scaled - 1.0) * inv_root_two  33.1 us
    reduce_sum x16, other arithmetic, payoff(): jnp.sum(weights[:, None] * state, axis=0) / jnp.sum(weights * spot_today)  31.9 us
    concatenate x32, local copies, waits for them, and re-layouts, basis_rows(): jnp.concatenate([leading, scaled, squares, neighbour, bounded], axis=0)  21.9 us
    reduce_sum x16, other arithmetic, path_state(): volatility[:, None] * (root_time * normals)  21.4 us
  transfers between devices with their start and end apart: 1, of which 1 were waited for; matrix products, arithmetic and copies ran while one was open for 0% of the time, Pallas kernels for 0%

commit v1 on v0

--- a/solution.py
+++ b/solution.py
@@ -80,7 +80,7 @@
     zero_gram = jnp.zeros((features, features), jnp.float32)
     zero_moment = jnp.zeros((2, features), jnp.float32)
     gram_acc, moment_acc = lax.fori_loop(0, block_count, gram_step, (zero_gram, zero_moment))
-    gram_sum, moment_sum = lax.psum((gram_acc, moment_acc), ("grp", "path"))
+    gram_sum, moment_sum = lax.psum(lax.psum((gram_acc, moment_acc), "grp"), "path")
     gram_mean = gram_sum / path_total
     moment_mean = moment_sum / path_total
     factor = jnp.linalg.cholesky(gram_mean)

time: 803 us -> 693 us (0.86)
  waiting for transfers between devices: 340 us -> 201 us
  blocking collectives: 213 us -> 242 us
    psum x1 -> x2, waiting for transfers between devices: 340 us -> 201 us  [the longest x1 122 us: per_device(): lax.psum(lax.psum((gram_acc, moment_acc), 'grp'), 'path')]
    psum x1 -> x2, blocking collectives: 111 us -> 131 us  [the longest x1 117 us: per_device(): lax.psum(lax.psum((gram_acc, moment_acc), 'grp'), 'path')]
    psum x1, blocking collectives: 101 us -> 111 us  [per_device(): greeks = lax.psum(greek_acc, ('grp', 'path')) / path_total]
  transfers between devices with their start and end apart: 1 -> 2, of which waited for: 1 -> 2; matrix products, arithmetic and copies ran while one was open for 0% -> 0% of each run, Pallas kernels for 0% -> 0%
where the time goes in v1:
time: 693 us; the launch traced here: 689 us
  blocking collectives  242 us (35%)
  waiting for transfers between devices  201 us (29%)
  other arithmetic  151 us (22%)
  local copies, waits for them, and re-layouts  40.1 us (6%)
  matrix products  24.6 us (4%)
  between operations  15.5 us (2%)
  loops' own time  14.4 us (2%)
    psum x1, waiting for transfers between devices, per_device(): lax.psum(lax.psum((gram_acc, moment_acc), 'grp'), 'path')  122 us
    psum x1, blocking collectives, per_device(): lax.psum(lax.psum((gram_acc, moment_acc), 'grp'), 'path')  117 us
    psum x1, blocking collectives, per_device(): greeks = lax.psum(greek_acc, ('grp', 'path')) / path_total  111 us
    psum x1, waiting for transfers between devices, per_device(): lax.psum((gram_acc, moment_acc), 'grp')  79.1 us
    mul x32, other arithmetic, basis_rows(): squares = (scaled * scaled - 1.0) * inv_root_two  33.1 us
    reduce_sum x16, other arithmetic, payoff(): jnp.sum(weights[:, None] * state, axis=0) / jnp.sum(weights * spot_today)  31.9 us
    concatenate x32, local copies, waits for them, and re-layouts, basis_rows(): jnp.concatenate([leading, scaled, squares, neighbour, bounded], axis=0)  21.9 us
    reduce_sum x16, other arithmetic, path_state(): volatility[:, None] * (root_time * normals)  21.4 us
  transfers between devices with their start and end apart: 2, of which 2 were waited for; matrix products, arithmetic and copies ran while one was open for 0% of the time, Pallas kernels for 0%

profile of v1, /device:TPU:1, one launch (start us, length us, event | category | flops | bytes accessed | tf_op | source)
XLA Modules:
  0.0 689.3 jit_solution(3964433449698811156)
XLA Ops:
  7.9 80.4 %while.42 = (s32[]{:T(128)}, f32[128,128]{1,0:T(8,128)S(1)}, f32[2,128]{1,0:T(2,128)S(1)}, f32[32]{0:T(128)}, f32[32,16384]{1,0:T(8,128)}, /*index=5*/f32[32]{0:...) while((s32[]{:T(128)}, f32[128,128]{1,0:T(8,128)S(1)}, ...), condition=%wide.region_1.2_spmd.clone, body=%wide.region_0.1_spmd.clone.sunk | while | flops 204870208 | bytes 3562582 | solution.py:82
  89.1 79.1 %all-reduce.6.cloned.1.call-done = f32[128,128]{0,1:T(8,128)} async-done(((f32[128,128]{0,1:T(8,128)}), f32[128,128]{0,1:T(8,128)}) %all-reduce.6.cloned.1.call-update) | async-done | bytes 65552 | tf_op jit(solution)/shard_map/psum | solution.py:83
  168.3 1.3 multiply_bitcast_fusion.2
  170.9 13.8 %psum.37 = f32[2,128]{1,0:T(2,128)S(1)} all-reduce(f32[2,128]{1,0:T(2,128)S(1)} %get-tuple-element.642), channel_id=1, replica_groups=mesh['grp'=8,'path'=64] {'grp'}, use_global_device_ids=true, to_apply=%region_6.7 | all-reduce | flops 256 | bytes 2048 | tf_op jit(solution)/shard_map/psum | solution.py:83
  184.7 116.9 %psum.38 = f32[2,128]{1,0:T(2,128)S(1)} all-reduce(f32[2,128]{1,0:T(2,128)S(1)} %psum.37), channel_id=1, replica_groups=mesh['grp'=8,'path'=64] {'path'}, use_global_device_ids=true, to_apply=%region_7.8 | all-reduce | flops 256 | bytes 2048 | tf_op jit(solution)/shard_map/psum | solution.py:83
  301.6 121.8 %all-reduce.8.cloned.1.call-done = f32[128,128]{0,1:T(8,128)} async-done(((f32[128,128]{0,1:T(8,128)}), f32[128,128]{0,1:T(8,128)}) %all-reduce.8.cloned.1.call-update) | async-done | bytes 65552 | tf_op jit(solution)/shard_map/psum | solution.py:83
  425.2 11.7 %cholesky.15 = f32[128,128]{1,0:T(8,128)S(1)} custom-call(f32[128,128]{1,0:T(8,128)S(1)} %fusion.19), custom_call_target="Cholesky" | custom-call | tf_op jit(solution)/shard_map/jit(cholesky)/cholesky | solution.py:86
  438.3 9.8 %custom-call.8 = f32[1,128,128]{1,2,0:T(8,128)S(1)} custom-call(f32[1,128,128]{2,1,0:T(8,128)S(1)} %fusion.14), custom_call_target="InvertDiagBlocksLowerTriangular" | custom-call | tf_op jit(solution)/shard_map/triangular_solve | solution.py:36
  448.8 121.5 %while.43 = (s32[]{:T(128)}, f32[16384]{0:T(1024)S(1)}, f32[32,16384]{1,0:T(8,128)S(1)}, f32[16384]{0:T(1024)S(1)}, f32[2,32]{1,0:T(2,128)S(1)}, /*index=5*/s32[...) while((s32[]{:T(128)}, f32[16384]{0:T(1024)S(1)}, ...), condition=%wide.region_17.18_spmd.clone, body=%wide.region_9.17_spmd.clone.sunk | while | flops 5333607 | bytes 5730625 | solution.py:138
  448.9 1.0 add_multiply_fusion.6
  451.4 2.0 multiply_reduce_fusion.8
  454.9 1.3 fusion.49
  456.5 1.0 add_multiply_fusion.6
  459.0 2.0 multiply_reduce_fusion.8
  462.5 1.3 fusion.49
  464.1 1.0 add_multiply_fusion.6
  466.6 2.0 multiply_reduce_fusion.8
  470.1 1.3 fusion.49
  471.7 1.0 add_multiply_fusion.6
  474.2 2.0 multiply_reduce_fusion.8
  477.7 1.3 fusion.49
  481.8 2.0 multiply_reduce_fusion.8
  485.3 1.3 fusion.49
  489.4 2.0 multiply_reduce_fusion.8
  492.9 1.3 fusion.49
  497.0 2.0 multiply_reduce_fusion.8
  500.5 1.3 fusion.49
  504.6 2.0 multiply_reduce_fusion.8
  508.1 1.3 fusion.49
  512.2 2.0 multiply_reduce_fusion.8
  515.7 1.3 fusion.49
  517.2 1.0 add_multiply_fusion.6
  519.8 2.0 multiply_reduce_fusion.8
  523.3 1.3 fusion.49
  527.4 2.0 multiply_reduce_fusion.8
  530.9 1.3 fusion.49
  535.0 2.0 multiply_reduce_fusion.8
  538.5 1.3 fusion.49
  542.6 2.0 multiply_reduce_fusion.8
  546.1 1.3 fusion.49
  550.2 2.0 multiply_reduce_fusion.8
  553.7 1.3 fusion.49
  555.2 1.0 add_multiply_fusion.6
  557.8 2.0 multiply_reduce_fusion.8
  561.3 1.3 fusion.49
  565.3 2.0 multiply_reduce_fusion.8
  568.9 1.3 fusion.49
  570.4 111.5 %psum.39 = f32[2,32]{1,0:T(2,128)S(1)} all-reduce(f32[2,32]{1,0:T(2,128)S(1)} %get-tuple-element.646), channel_id=1, replica_groups=mesh['grp'=8,'path'=64] {'grp','path'}, use_global_device_ids=true, to_apply=%region_18.19 | all-reduce | flops 64 | bytes 512 | tf_op jit(solution)/shard_map/psum | solution.py:141
  (540 shorter events, 133.9 us)
Async XLA Ops:
  7.2 161.1 %all-reduce.6.cloned.1.call-start = ((), (), s32[]{:S(2)}) async-start(), calls=%async_computation | async-start | bytes 131072 | tf_op jit(solution)/shard_map/psum | solution.py:83
  7.9 160.4 %copy-start.1 = (f32[32]{0:T(128)S(1)}, f32[32]{0:T(128)}, u32[]{:S(2)}) copy-start(f32[32]{0:T(128)} %param.13) | copy-start | bytes 388
  88.3 360.5 %copy-start.2 = (f32[32]{0:T(128)S(1)}, f32[32]{0:T(128)}, u32[]{:S(2)}) copy-start(f32[32]{0:T(128)} %get-tuple-element.1154) | copy-start | bytes 388
  88.3 360.5 %copy-start.5 = (f32[32]{0:T(128)S(1)}, f32[32]{0:T(128)}, u32[]{:S(2)}) copy-start(f32[32]{0:T(128)} %get-tuple-element.1158) | copy-start | bytes 388
  89.1 334.3 %all-reduce.8.cloned.1.call-start = ((), (), s32[]{:S(2)}) async-start(), calls=%async_computation.1 | async-start | bytes 131072 | tf_op jit(solution)/shard_map/psum | solution.py:83
  570.3 112.1 %copy-start = (f32[32,16384]{1,0:T(8,128)}, f32[32,16384]{1,0:T(8,128)S(1)}, u32[]{:S(2)}) copy-start(f32[32,16384]{1,0:T(8,128)S(1)} %get-tuple-element.638) | copy-start | bytes 6291460
  570.4 112.1 %copy-start.3 = (f32[16384]{0:T(1024)}, f32[16384]{0:T(1024)S(1)}, u32[]{:S(2)}) copy-start(f32[16384]{0:T(1024)S(1)} %get-tuple-element.639) | copy-start | bytes 196612
  570.4 112.0 %copy-start.4 = (f32[16384]{0:T(1024)}, f32[16384]{0:T(1024)S(1)}, u32[]{:S(2)}) copy-start(f32[16384]{0:T(1024)S(1)} %get-tuple-element.637) | copy-start | bytes 196612
Sparse Core Ops, SparseCore 0:
  89.2 79.0 all-reduce.5
  171.7 251.6 all-reduce.7
